TPU v7x, 32 devices: a whole 2x2x4 slice. The times are simulated.
32 devices in a mesh: row: 8 (over y, x, core), vec: 4 (over z).
Axes of the slice: x: 2, y: 2, z: 4, core: 2. Of those that a mesh axis runs over, the one named last changes fastest.
Arguments:
- ham_tiles: bfloat16 [512, 4, 128, 128], P('row'), may hold values from -0.125 to 0.125
- tile_columns: int32 [512, 4], P('row'), may hold values from 0 to 511, as said below
- stack_lengths: int32 [8], P('row'), may hold values from 32 to 64, as said below
- start_vectors: bfloat16 [65536, 1024], P('row', 'vec'), may hold values from -6 to 6
- spectral_scale: float32 [1], replicated, may hold values from 4 to 16
Outputs:
- filtered_basis: bfloat16 [65536, 1024], P('row', 'vec')
Inputs may be any that keep to these rules, and one draw needn't show every extreme that they name: `tile_columns`: row b lists 4 distinct block columns; the first is b itself, the others are (b + o) mod 512 with nonzero offsets o from -2 to 2. Some stack holds 64 occupied block rows and some other stack exactly half of 64; a stack's occupied rows are its first stack_lengths - 2 and its last 2 block rows.
All inputs are finite; a program needn't handle non-finite values.
Results may differ from a plain program's by a relative error of at most 0.006.
The roundings to bfloat16 on the way count: a program that leaves them out, or rounds other values in their place, can miss the bound.
Values may be sent and summed in bfloat16 or wider, within the bound.
A program may use at most 128 MiB of HBM per device.

v0:
```python
import jax
import jax.numpy as jnp
from jax import lax
from jax.sharding import PartitionSpec as P

REACH = 2
CHEB = 6
NS_ITERS = 2


def with_halo(block, sides, width):
    for axis, dim in sides:
        count = lax.axis_size(axis)
        forward = [(i, i + 1) for i in range(count - 1)]
        forward.append((count - 1, 0))
        backward = [(target, source) for source, target in forward]
        low = lax.ppermute(
            lax.slice_in_dim(block, block.shape[dim] - width, None, axis=dim), axis, forward
        )
        high = lax.ppermute(lax.slice_in_dim(block, 0, width, axis=dim), axis, backward)
        block = jnp.concatenate([low, block, high], axis=dim)
    return block


def local(ham_tiles, tile_columns, stack_lengths, start_vectors, spectral_scale):
    row_count, panel_width = start_vectors.shape
    block_count = ham_tiles.shape[0]
    tile_size = ham_tiles.shape[2]
    total_blocks = block_count * lax.axis_size("row")
    total_rows = row_count * lax.axis_size("row")
    full_width = panel_width * lax.axis_size("vec")
    first_block = lax.axis_index("row") * block_count
    block_ids = first_block + jnp.arange(block_count, dtype=jnp.int32)
    offsets = (tile_columns - block_ids[:, None] + REACH) % total_blocks - REACH
    local_ids = jnp.arange(block_count, dtype=jnp.int32)[:, None] + offsets + REACH
    local_rows = jnp.arange(block_count, dtype=jnp.int32)
    live = (local_rows < stack_lengths[0] - REACH) | (local_rows >= block_count - REACH)
    live_mask = live.astype(jnp.float32)[:, None, None]

    def apply_hamiltonian(current):
        blocked = current.reshape(block_count, tile_size, panel_width)
        padded = with_halo(blocked, (("row", 0),), REACH)
        picked = padded[local_ids]
        product = jnp.einsum(
            "btij,btjc->bic", ham_tiles, picked, preferred_element_type=jnp.float32
        )
        return (product * live_mask).reshape(row_count, panel_width)

    earlier = start_vectors
    current = apply_hamiltonian(start_vectors).astype(jnp.bfloat16)
    for repeat in range(CHEB - 1):
        following = (2.0 * apply_hamiltonian(current) - earlier.astype(jnp.float32)).astype(
            jnp.bfloat16
        )
        earlier, current = (current, following)
    panel_rows = lax.all_to_all(current, "vec", split_axis=0, concat_axis=1, tiled=True)
    partial_gram = lax.dot_general(
        panel_rows, panel_rows, (((0,), (0,)), ((), ())), preferred_element_type=jnp.float32
    ) / float(total_rows)
    gram = lax.psum(partial_gram, ("row", "vec"))
    scale = spectral_scale[0] * jnp.trace(gram) / full_width
    system = gram / scale
    root = jnp.eye(full_width, dtype=jnp.float32)
    for repeat in range(NS_ITERS):
        product_w = jnp.dot(system, root, precision=lax.Precision.HIGHEST)
        product_p = jnp.dot(product_w, root, precision=lax.Precision.HIGHEST)
        root = 1.5 * root - 0.5 * jnp.dot(product_p, root, precision=lax.Precision.HIGHEST)
    weights = (root / jnp.sqrt(scale)).astype(jnp.bfloat16)
    basis_rows = jnp.dot(panel_rows, weights, preferred_element_type=jnp.float32).astype(
        jnp.bfloat16
    )
    return lax.all_to_all(basis_rows, "vec", split_axis=1, concat_axis=0, tiled=True)


def solution(mesh):
    placed = (P("row", None, None, None), P("row", None), P("row"), P("row", "vec"), P())
    return jax.shard_map(
        local, mesh=mesh, in_specs=placed, out_specs=P("row", "vec"), check_vma=False
    )
```

profile of v0, /device:TPU:9, one launch (start us, length us, event | category | flops | bytes accessed | tf_op | source)
XLA Modules:
  0.0 697.7 jit_solution(11538666851263681071)
XLA Ops:
  18.3 12.0 %gather_fusion = bf16[256,128,256]{2,1,0:T(8,128)(2,1)} fusion(bf16[68,128,256]{2,1,0:T(8,128)(2,1)} %pad_maximum_fusion, s32[1024]{0:T(1024)S(1)} %pad_clamp_fusion), kind=kCustom, calls=%fused_computation | custom fusion | bytes 33555456 | tf_op jit(solution)/shard_map/gather | solution.py:43
  30.3 12.2 %fusion.14 = bf16[64,128,256]{1,2,0:T(8,128)(2,1)} fusion(f32[64]{0:T(128)S(1)} %or_convert_fusion, bf16[64,4,128,256]{3,2,1,0:T(8,128)(2,1)} %bitcast.115, bf16[64,4,128,128]{3,2,1,0:T(8,128)(2,1)} %param.5), kind=kOutput, calls=%fused_computation.37 | convolution fusion | flops 2151677952 | bytes 29360384 | tf_op jit(solution)/shard_map/btij,btjc->bic/dot_general | solution.py:44
  53.4 12.0 %gather_fusion.1 = bf16[256,128,256]{1,2,0:T(8,128)(2,1)} fusion(bf16[68,128,256]{1,2,0:T(8,128)(2,1)} %pad_maximum_fusion.1, s32[1024]{0:T(1024)S(1)} %pad_clamp_fusion), kind=kCustom, calls=%fused_computation.1 | custom fusion | bytes 33555456 | tf_op jit(solution)/shard_map/gather | solution.py:43
  65.4 12.5 %fusion.12 = f32[64,128,256]{1,2,0:T(8,128)} fusion(f32[64]{0:T(128)S(1)} %or_convert_fusion, bf16[64,4,128,256]{2,3,1,0:T(8,128)(2,1)} %bitcast.122, bf16[64,4,128,128]{3,2,1,0:T(8,128)(2,1)} %param.5), kind=kOutput, calls=%fused_computation.28 | convolution fusion | flops 2151677952 | bytes 33554688 | tf_op jit(solution)/shard_map/btij,btjc->bic/dot_general | solution.py:44
  77.9 9.0 %copy.20 = f32[64,128,256]{2,1,0:T(8,128)} copy(f32[64,128,256]{1,2,0:T(8,128)} %fusion.12) | data formatting | bytes 16777216 | tf_op jit(solution)/shard_map/mul | solution.py:52
  87.0 5.6 fusion.10
  100.9 12.0 %gather_fusion.2 = bf16[256,128,256]{2,1,0:T(8,128)(2,1)} fusion(bf16[68,128,256]{2,1,0:T(8,128)(2,1)} %pad_maximum_fusion.2, s32[1024]{0:T(1024)S(1)} %pad_clamp_fusion), kind=kCustom, calls=%fused_computation.2 | custom fusion | bytes 33555456 | tf_op jit(solution)/shard_map/gather | solution.py:43
  112.9 12.0 %fusion.8 = bf16[64,128,256]{1,2,0:T(8,128)(2,1)S(1)} fusion(bf16[64,128,256]{1,2,0:T(8,128)(2,1)} %fusion.14, f32[64]{0:T(128)S(1)} %or_convert_fusion, bf16[64,4,128,256]{3,2,1,0:T(8,128)(2,1)} %bitcast.120, bf16[64,4,128,128]{3,2,1,0:T(8,128)(2,1)} %param.5), kind=kOutput, calls=%fused_computation.21 | convolution fusion | flops 2157969408 | bytes 33554688 | tf_op jit(solution)/shard_map/btij,btjc->bic/dot_general | solution.py:44
  134.2 12.0 %gather_fusion.3 = bf16[256,128,256]{1,2,0:T(8,128)(2,1)} fusion(bf16[68,128,256]{1,2,0:T(8,128)(2,1)} %pad_maximum_fusion.3, s32[1024]{0:T(1024)S(1)} %pad_clamp_fusion), kind=kCustom, calls=%fused_computation.3 | custom fusion | bytes 33555456 | tf_op jit(solution)/shard_map/gather | solution.py:43
  146.2 12.5 %fusion.7 = f32[64,128,256]{1,2,0:T(8,128)} fusion(f32[64]{0:T(128)S(1)} %or_convert_fusion, bf16[64,4,128,256]{2,3,1,0:T(8,128)(2,1)} %bitcast.123, bf16[64,4,128,128]{3,2,1,0:T(8,128)(2,1)} %param.5), kind=kOutput, calls=%fused_computation.19 | convolution fusion | flops 2151677952 | bytes 33554688 | tf_op jit(solution)/shard_map/btij,btjc->bic/dot_general | solution.py:44
  158.7 9.0 %copy.24 = f32[64,128,256]{2,1,0:T(8,128)} copy(f32[64,128,256]{1,2,0:T(8,128)} %fusion.7) | data formatting | bytes 16777216 | tf_op jit(solution)/shard_map/mul | solution.py:52
  167.8 5.6 fusion.5
  173.5 11.5 %collective-permute-start.9 = (bf16[2,128,256]{2,1,0:T(8,128)(2,1)S(1)}, bf16[2,128,256]{2,1,0:T(8,128)(2,1)S(1)}, u32[]{:S(2)}, u32[]{:S(2)}) collective-permute-start(bf16[2,128,256]{2,1,0:T(8,128)(2,1)S(1)} %bitcast.132), channel_id=1, source_target_pairs={{4,0},{8,4},{12,8},{16,12},{20,16},{24,20},{28,24},{0,28},{5,1},{9... | collective-permute-start | bytes 393224 | tf_op jit(solution)/shard_map/ppermute | solution.py:20
  191.7 12.0 %gather_fusion.4 = bf16[256,128,256]{2,1,0:T(8,128)(2,1)} fusion(bf16[68,128,256]{2,1,0:T(8,128)(2,1)} %pad_maximum_fusion.4, s32[1024]{0:T(1024)S(1)} %pad_clamp_fusion), kind=kCustom, calls=%fused_computation.4 | custom fusion | bytes 33555456 | tf_op jit(solution)/shard_map/gather | solution.py:43
  203.7 12.0 %fusion.3 = bf16[64,128,256]{1,2,0:T(8,128)(2,1)S(1)} fusion(bf16[64,128,256]{1,2,0:T(8,128)(2,1)} %copy-done.2, f32[64]{0:T(128)S(1)} %or_convert_fusion, bf16[64,4,128,256]{3,2,1,0:T(8,128)(2,1)} %bitcast.121, bf16[64,4,128,128]{3,2,1,0:T(8,128)(2,1)} %param.5), kind=kOutput, calls=%fused_computation.12 | convolution fusion | flops 2157969408 | bytes 33554688 | tf_op jit(solution)/shard_map/btij,btjc->bic/dot_general | solution.py:44
  217.7 5.3 collective-permute-done.11
  225.4 12.0 %gather_fusion.5 = bf16[256,128,256]{1,2,0:T(8,128)(2,1)} fusion(bf16[68,128,256]{1,2,0:T(8,128)(2,1)} %pad_maximum_fusion.5, s32[1024]{0:T(1024)S(1)} %pad_clamp_fusion), kind=kCustom, calls=%fused_computation.5 | custom fusion | bytes 33555456 | tf_op jit(solution)/shard_map/gather | solution.py:43
  237.5 12.5 %fusion.2 = f32[64,128,256]{1,2,0:T(8,128)} fusion(f32[64]{0:T(128)S(1)} %or_convert_fusion, bf16[64,4,128,256]{2,3,1,0:T(8,128)(2,1)} %bitcast.119, bf16[64,4,128,128]{3,2,1,0:T(8,128)(2,1)} %param.5), kind=kOutput, calls=%fused_computation.10 | convolution fusion | flops 2151677952 | bytes 33554688 | tf_op jit(solution)/shard_map/btij,btjc->bic/dot_general | solution.py:44
  250.0 9.0 %copy.28 = f32[64,128,256]{2,1,0:T(8,128)} copy(f32[64,128,256]{1,2,0:T(8,128)} %fusion.2) | data formatting | bytes 16777216 | tf_op jit(solution)/shard_map/mul | solution.py:52
  259.0 7.6 %fusion = bf16[8192,256]{1,0:T(8,128)(2,1)} fusion(f32[64,128,256]{2,1,0:T(8,128)} %copy.28, bf16[8192,256]{1,0:T(8,128)(2,1)} %copy-done), kind=kLoop, calls=%fused_computation.7 | loop fusion | flops 6291456 | bytes 16777216 | tf_op jit(solution)/shard_map/convert_element_type | solution.py:52
  266.6 6.3 copy.29
  272.9 95.4 %all_to_all.38 = bf16[4,2048,256]{1,2,0:T(8,128)(2,1)S(1)} all-to-all(bf16[4,2048,256]{1,2,0:T(8,128)(2,1)} %copy.29), channel_id=1, replica_groups=mesh['row'=8,'vec'=4] {'vec'}, dimensions={0} | all-to-all | bytes 8388608 | tf_op jit(solution)/shard_map/all_to_all | solution.py:56
  370.2 6.1 convolution_multiply_fusion
  377.0 139.6 %all-reduce.2.cloned.1.call-done = f32[1024,1024]{1,0:T(8,128)} async-done(((f32[1024,1024]{1,0:T(8,128)}), f32[1024,1024]{1,0:T(8,128)}) %all-reduce.2.cloned.1.call-update) | async-done | bytes 4194320 | tf_op jit(solution)/shard_map/psum | solution.py:60
  520.4 8.9 %fusion.17 = f32[1024,1024]{1,0:T(8,128)S(1)} fusion(f32[1024,1024]{1,0:T(8,128)} %all-reduce.2.cloned.1.call-done, f32[]{:T(128)S(6)} %div.23), kind=kOutput, calls=%fused_computation.44 | convolution fusion | flops 12886999040 | bytes 8388612 | tf_op jit(solution)/shard_map/dot_general | solution.py:65
  529.3 6.7 fusion.16
  535.9 6.8 fusion.15
  542.7 13.7 %fusion.19 = f32[1024,1024]{1,0:T(8,128)S(1)} fusion(f32[1024,1024]{1,0:T(8,128)S(1)} %fusion.15, f32[1024,1024]{1,0:T(8,128)S(1)} %copy-done.5, f32[]{:T(128)S(6)} %div.23), kind=kOutput, calls=%fused_computation.48 | convolution fusion | flops 12890144768 | bytes 12582916 | tf_op jit(solution)/shard_map/dot_general | solution.py:65
  556.4 13.7 %fusion.18 = f32[1024,1024]{1,0:T(8,128)S(1)} fusion(f32[1024,1024]{1,0:T(8,128)S(1)} %fusion.19, f32[1024,1024]{1,0:T(8,128)S(1)} %fusion.15), kind=kOutput, calls=%fused_computation.47 | convolution fusion | flops 12889096192 | bytes 12582912 | tf_op jit(solution)/shard_map/dot_general | solution.py:66
  570.2 14.7 %divide_convert_fusion = bf16[1024,1024]{1,0:T(8,128)(2,1)S(1)} fusion(f32[1024,1024]{1,0:T(8,128)S(1)} %fusion.18, f32[1024,1024]{1,0:T(8,128)S(1)} %fusion.15, f32[]{:T(128)S(6)} %sqrt.3), kind=kOutput, calls=%fused_computation.38 | convolution fusion | flops 12898533376 | bytes 10485764 | tf_op jit(solution)/shard_map/dot_general | solution.py:67
  590.0 94.2 %all_to_all.39 = bf16[2048,4,256]{0,2,1:T(8,128)(2,1)} all-to-all(bf16[2048,4,256]{0,2,1:T(8,128)(2,1)S(1)} %bitcast.128), channel_id=1, replica_groups=mesh['row'=8,'vec'=4] {'vec'}, dimensions={1} | all-to-all | bytes 8388608 | tf_op jit(solution)/shard_map/all_to_all | solution.py:72
  684.2 6.2 copy.30
  (56 shorter events, 60.7 us)
Async XLA Ops:
  6.5 510.1 %all-reduce.2.cloned.1.call-start = ((), (), s32[]{:S(2)}) async-start(), calls=%async_computation.2 | async-start | bytes 8388608 | tf_op jit(solution)/shard_map/psum | solution.py:60
  7.5 3.8 collective-permute-start
  9.3 5.0 collective-permute-start.1
  43.5 2.0 collective-permute-start.2
  43.6 5.9 collective-permute-start.3
  92.5 6.0 copy-start.1
  92.6 2.0 collective-permute-start.4
  92.6 5.8 collective-permute-start.5
  124.9 6.9 copy-start.2
  124.9 2.0 collective-permute-start.6
  125.0 6.8 collective-permute-start.7
  173.4 15.9 %copy-start = (bf16[8192,256]{1,0:T(8,128)(2,1)}, bf16[8192,256]{1,0:T(8,128)(2,1)S(1)}, u32[]{:S(2)}) copy-start(bf16[8192,256]{1,0:T(8,128)(2,1)S(1)} %fusion.5) | copy-start | bytes 12582916
  173.4 11.6 %collective-permute-start.8 = (bf16[2,128,256]{2,1,0:T(8,128)(2,1)S(1)}, bf16[2,128,256]{2,1,0:T(8,128)(2,1)S(1)}, u32[]{:S(2)}, u32[]{:S(2)}) collective-permute-start(bf16[2,128,256]{2,1,0:T(8,128)(2,1)S(1)} %bitcast.134), channel_id=1, source_target_pairs={{0,4},{4,8},{8,12},{12,16},{16,20},{20,24},{24,28},{28,0},{1,5},{5... | collective-permute-start | bytes 393224 | tf_op jit(solution)/shard_map/ppermute | solution.py:17
  173.5 15.8 %collective-permute-start.9 = (bf16[2,128,256]{2,1,0:T(8,128)(2,1)S(1)}, bf16[2,128,256]{2,1,0:T(8,128)(2,1)S(1)}, u32[]{:S(2)}, u32[]{:S(2)}) collective-permute-start(bf16[2,128,256]{2,1,0:T(8,128)(2,1)S(1)} %bitcast.132), channel_id=1, source_target_pairs={{4,0},{8,4},{12,8},{16,12},{20,16},{24,20},{28,24},{0,28},{5,1},{9... | collective-permute-start | bytes 393224 | tf_op jit(solution)/shard_map/ppermute | solution.py:20
  215.7 2.0 collective-permute-start.10
  215.8 7.3 %collective-permute-start.11 = (bf16[2,128,256]{1,2,0:T(8,128)(2,1)S(1)}, bf16[2,128,256]{1,2,0:T(8,128)(2,1)S(1)}, u32[]{:S(2)}, u32[]{:S(2)}) collective-permute-start(bf16[2,128,256]{1,2,0:T(8,128)(2,1)S(1)} %get-tuple-element.6), channel_id=1, source_target_pairs={{4,0},{8,4},{12,8},{16,12},{20,16},{24,20},{28,24},{0,28},{5,1},{9... | collective-permute-start | bytes 393224 | tf_op jit(solution)/shard_map/ppermute | solution.py:20
  368.2 2.0 copy-start.3
  535.9 6.8 copy-start.5
  570.2 14.8 %copy-start.4 = (bf16[4,2048,256]{1,2,0:T(8,128)(2,1)S(1)}, bf16[4,2048,256]{1,2,0:T(8,128)(2,1)}, u32[]{:S(2)}) copy-start(bf16[4,2048,256]{1,2,0:T(8,128)(2,1)} %copy-done.3) | copy-start | bytes 12582916
Sparse Core Ops, SparseCore 0:
  376.5 140.1 all-reduce.1
where the time goes:
time: 711 us; the launch traced here: 698 us
  blocking collectives  190 us (27%)
  waiting for transfers between devices  171 us (24%)
  matrix products  149 us (21%)
  local copies, waits for them, and re-layouts  116 us (16%)
  other arithmetic  39.8 us (6%)
  between operations  16.1 us (2%)
  starting transfers between devices  15.9 us (2%)
    psum x1, waiting for transfers between devices, local(): gram = lax.psum(partial_gram, ('row', 'vec'))  140 us
    all_to_all x1, blocking collectives, local(): lax.all_to_all(current, 'vec', split_axis=0, concat_axis=1, tiled=True)  95.4 us
    all_to_all x1, blocking collectives, local(): lax.all_to_all(basis_rows, 'vec', split_axis=1, concat_axis=0, tiled=True)  94.2 us
    dot_general x6, matrix products, apply_hamiltonian(): jnp.einsum('btij,btjc->bic', ham_tiles, picked, preferred_element_type=jn...  73.7 us
    gather x6, local copies, waits for them, and re-layouts, apply_hamiltonian(): picked = padded[local_ids]  72.2 us
    mul x3, local copies, waits for them, and re-layouts, local(): 2.0 * apply_hamiltonian(current) - earlier.astype(jnp.float32)  27.1 us
    ppermute x6, waiting for transfers between devices, with_halo(): lax.ppermute(lax.slice_in_dim(block, 0, width, axis=dim), axis, backward)  25.4 us
    dot_general x2, matrix products, local(): product_w = jnp.dot(system, root, precision=lax.Precision.HIGHEST)  22.6 us
  transfers between devices with their start and end apart: 13, of which 12 were waited for; matrix products, arithmetic and copies ran while one was open for 0% of the time, Pallas kernels for 0%

commit v1 on v0

v1 whole, which is shorter than its diff:
```python
import functools

import jax
import jax.numpy as jnp
from jax import lax
from jax.experimental import pallas as pl
from jax.experimental.pallas import tpu as pltpu
from jax.sharding import PartitionSpec as P

REACH = 2
CHEB = 6


def chebyshev_kernel(
    total_blocks,
    columns_ref,
    lengths_ref,
    tiles_ref,
    start_ref,
    out_ref,
    band,
    even,
    odd,
    halo,
    send_sem,
    recv_sem,
):
    block_count, tile_count, tile, _ = tiles_ref.shape
    pair = REACH * tile
    pairs = block_count // REACH
    count = lax.axis_size("row")
    me = lax.axis_index("row")
    left, right = lax.rem(me + count - 1, count), lax.rem(me + 1, count)
    last = (pairs - 1) * pair

    barrier = pltpu.get_barrier_semaphore()
    for neighbour in (left, right):
        pl.semaphore_signal(
            barrier, inc=1, device_id={"row": neighbour}, device_id_type=pl.DeviceIdType.MESH
        )
    pl.semaphore_wait(barrier, 2)

    def sends(source, step):
        to_left = pltpu.make_async_remote_copy(
            src_ref=source.at[pl.ds(0, pair)],
            dst_ref=halo.at[step, 1],
            send_sem=send_sem.at[step, 1],
            recv_sem=recv_sem.at[step, 1],
            device_id={"row": left},
            device_id_type=pl.DeviceIdType.MESH,
        )
        to_right = pltpu.make_async_remote_copy(
            src_ref=source.at[pl.ds(last, pair)],
            dst_ref=halo.at[step, 0],
            send_sem=send_sem.at[step, 0],
            recv_sem=recv_sem.at[step, 0],
            device_id={"row": right},
            device_id_type=pl.DeviceIdType.MESH,
        )
        return to_left, to_right

    copies = sends(start_ref, 0)
    for copy in copies:
        copy.start()

    def build(p, carry):
        for i in range(REACH):
            b = p * REACH + i
            live = (b < lengths_ref[0] - REACH) | (b >= block_count - REACH)
            places = []
            for t in range(tile_count):
                shift = lax.rem(
                    columns_ref[b * tile_count + t] - (me * block_count + b) + REACH + total_blocks,
                    total_blocks,
                )
                places.append(jnp.where(live, shift, -1))
            for c in range(3 * REACH):
                value = None
                if 0 <= c - i <= 2 * REACH:
                    for t in range(tile_count):
                        hit = jnp.where(places[t] == c - i, 1.0, 0.0).astype(jnp.float32)
                        mask = jnp.full((tile, tile), hit, jnp.float32).astype(jnp.bfloat16)
                        term = tiles_ref[b, t] * mask
                        value = term if value is None else value + term
                else:
                    value = jnp.zeros((tile, tile), jnp.bfloat16)
                band[p, i * tile : (i + 1) * tile, c * tile : (c + 1) * tile] = value
        return carry

    lax.fori_loop(0, pairs, build, 0)

    held = [start_ref, odd, even, odd, even, odd, out_ref]
    for step in range(CHEB):
        current, target = held[step], held[step + 1]
        earlier = held[step - 1] if step else None

        def finish(product, rows):
            if earlier is not None:
                product = 2.0 * product - earlier[rows, :].astype(jnp.float32)
            target[rows, :] = product.astype(jnp.bfloat16)

        for copy in copies:
            copy.wait()
        top = pl.ds(0, pair)
        finish(
            jnp.dot(band[0, :, :pair], halo[step, 0], preferred_element_type=jnp.float32)
            + jnp.dot(
                band[0, :, pair:], current[0 : 2 * pair, :], preferred_element_type=jnp.float32
            ),
            top,
        )
        finish(
            jnp.dot(
                band[pairs - 1, :, 2 * pair :], halo[step, 1], preferred_element_type=jnp.float32
            )
            + jnp.dot(
                band[pairs - 1, :, : 2 * pair],
                current[last - pair : last + pair, :],
                preferred_element_type=jnp.float32,
            ),
            pl.ds(last, pair),
        )

        def interior(p, carry):
            before = pl.multiple_of((p - 1) * pair, pair)
            here = pl.multiple_of(p * pair, pair)
            finish(
                jnp.dot(
                    band[p], current[pl.ds(before, 3 * pair), :], preferred_element_type=jnp.float32
                ),
                pl.ds(here, pair),
            )
            return carry

        early = min(7, pairs - 1)
        lax.fori_loop(1, early, interior, 0, unroll=3)
        if step < CHEB - 1:
            copies = sends(target, step + 1)
            for copy in copies:
                copy.start()
        lax.fori_loop(early, pairs - 1, interior, 0, unroll=4)


def chebyshev(ham_tiles, tile_columns, stack_lengths, start_vectors):
    block_count, tile_count, tile, _ = ham_tiles.shape
    rows, width = start_vectors.shape
    pair = REACH * tile
    vmem = pl.BlockSpec(memory_space=pltpu.VMEM)
    smem = pl.BlockSpec(memory_space=pltpu.SMEM)
    return pl.pallas_call(
        functools.partial(chebyshev_kernel, block_count * lax.axis_size("row")),
        out_shape=jax.ShapeDtypeStruct((rows, width), jnp.bfloat16),
        in_specs=[smem, smem, vmem, vmem],
        out_specs=vmem,
        scratch_shapes=[
            pltpu.VMEM((block_count // REACH, pair, 3 * pair), jnp.bfloat16),
            pltpu.VMEM((rows, width), jnp.bfloat16),
            pltpu.VMEM((rows, width), jnp.bfloat16),
            pltpu.VMEM((CHEB, 2, pair, width), jnp.bfloat16),
            pltpu.SemaphoreType.DMA((CHEB, 2)),
            pltpu.SemaphoreType.DMA((CHEB, 2)),
        ],
        compiler_params=pltpu.CompilerParams(
            collective_id=0, has_side_effects=True, vmem_limit_bytes=60 * 1024 * 1024
        ),
    )(tile_columns.reshape(-1), stack_lengths, ham_tiles, start_vectors)


def local(ham_tiles, tile_columns, stack_lengths, start_vectors, spectral_scale):
    row_count, panel_width = start_vectors.shape
    total_rows = row_count * lax.axis_size("row")
    full_width = panel_width * lax.axis_size("vec")
    current = chebyshev(ham_tiles, tile_columns, stack_lengths, start_vectors)
    panel_rows = lax.all_to_all(current, "vec", split_axis=0, concat_axis=1, tiled=True)

    part = 256
    parts = full_width // part
    packed = jnp.concatenate(
        [
            lax.dot_general(
                panel_rows[:, j * part : (j + 1) * part],
                panel_rows[:, : (j + 1) * part],
                (((0,), (0,)), ((), ())),
                preferred_element_type=jnp.float32,
            )
            for j in range(parts)
        ],
        axis=1,
    )
    packed = lax.psum(packed / float(total_rows), ("row", "vec"))
    starts = [j * (j + 1) // 2 * part for j in range(parts)]

    def block(i, j):
        if j <= i:
            return packed[:, starts[i] + j * part : starts[i] + (j + 1) * part]
        return block(j, i).T

    gram = jnp.concatenate(
        [jnp.concatenate([block(i, j) for j in range(parts)], axis=1) for i in range(parts)], axis=0
    )
    scale = spectral_scale[0] * jnp.trace(gram) / full_width
    system = gram / scale
    identity = jnp.eye(full_width, dtype=jnp.float32)
    square = jnp.dot(system, system, precision=lax.Precision.HIGH)
    first = 1.5 * identity - 0.5 * system
    left = 1.5 * system - 0.5 * square
    right = 2.25 * identity - 1.5 * system + 0.25 * square
    root = 1.5 * first - 0.5 * jnp.dot(left, right, precision=lax.Precision.HIGH)
    weights = (root / jnp.sqrt(scale)).astype(jnp.bfloat16)
    basis_rows = jnp.dot(panel_rows, weights, preferred_element_type=jnp.float32).astype(
        jnp.bfloat16
    )
    return lax.all_to_all(basis_rows, "vec", split_axis=1, concat_axis=0, tiled=True)


def solution(mesh):
    placed = (P("row", None, None, None), P("row", None), P("row"), P("row", "vec"), P())
    return jax.shard_map(
        local, mesh=mesh, in_specs=placed, out_specs=P("row", "vec"), check_vma=False
    )
```

time: 711 us -> 461 us (0.65); the launches traced: 698 us -> 456 us
  matrix products: 149 us -> 35.7 us
  local copies, waits for them, and re-layouts: 116 us -> 26.3 us
  Pallas kernels: 0 us -> 46.2 us
  other arithmetic: 39.8 us -> 4.51 us
  waiting for transfers between devices: 171 us -> 138 us
  starting transfers between devices: 15.9 us -> 0.01 us
    dot_general x13 -> x6, matrix products: 144 us -> 28.3 us  [the longest x1 13.1 us: local(): jnp.dot(left, right, precision=lax.Precision.HIGH)]
    gather x6 -> x0, local copies, waits for them, and re-layouts: 72.2 us -> none  [apply_hamiltonian(): picked = padded[local_ids]]
    pallas_call x0 -> x1, Pallas kernels: none -> 46.2 us  [chebyshev(): pl.pallas_call(functools.partial(chebyshev_kernel, block_count * lax.axis...]
    ppermute x12 -> x0, waiting for transfers between devices: 31.3 us -> none  [the longest x6 25.4 us: with_halo(): lax.ppermute(lax.slice_in_dim(block, 0, width, axis=dim), axis, backward)]
    mul x3 -> x0, local copies, waits for them, and re-layouts: 27.1 us -> none  [local(): 2.0 * apply_hamiltonian(current) - earlier.astype(jnp.float32)]
    convert_element_type x4 -> x0, other arithmetic: 18.7 us -> none  [the longest x3 18.7 us: local(): (2.0 * apply_hamiltonian(current) - earlier.astype(jnp.float32)).astype(j...]
    concatenate x6 -> x0, other arithmetic: 17.4 us -> none  [with_halo(): block = jnp.concatenate([low, block, high], axis=dim)]
    ppermute x12 -> x0, starting transfers between devices: 15.9 us -> none  [the longest x6 13.7 us: with_halo(): lax.ppermute(lax.slice_in_dim(block, 0, width, axis=dim), axis, backward)]
  transfers between devices with their start and end apart: 13 -> 1, of which waited for: 12 -> 1; matrix products, arithmetic and copies ran while one was open for 0% -> 0% of each run, Pallas kernels for 0% -> 0%
where the time goes in v1:
time: 461 us; the launch traced here: 456 us
  blocking collectives  189 us (41%)
  waiting for transfers between devices  138 us (30%)
  Pallas kernels  46.2 us (10%)
  matrix products  35.7 us (8%)
  local copies, waits for them, and re-layouts  26.3 us (6%)
  between operations  15.6 us (3%)
    psum x1, waiting for transfers between devices, local(): packed = lax.psum(packed / float(total_rows), ('row', 'vec'))  138 us
    all_to_all x1, blocking collectives, local(): lax.all_to_all(basis_rows, 'vec', split_axis=1, concat_axis=0, tiled=True)  95 us
    all_to_all x1, blocking collectives, local(): lax.all_to_all(current, 'vec', split_axis=0, concat_axis=1, tiled=True)  94.4 us
    pallas_call x1, Pallas kernels, chebyshev(): pl.pallas_call(functools.partial(chebyshev_kernel, block_count * lax.axis...  46.2 us
    dot_general x1, matrix products, local(): jnp.dot(left, right, precision=lax.Precision.HIGH)  13.1 us
    dot_general x1, matrix products, local(): square = jnp.dot(system, system, precision=lax.Precision.HIGH)  11.7 us
    unnamed x41, local copies, waits for them, and re-layouts  10.4 us
  transfers between devices with their start and end apart: 1, of which 1 were waited for; matrix products, arithmetic and copies ran while one was open for 0% of the time, Pallas kernels for 0%

profile of v1, /device:TPU:9, one launch (start us, length us, event | category | flops | bytes accessed | tf_op | source)
XLA Modules:
  0.0 455.7 jit_solution(11179723673710536511)
XLA Ops:
  7.2 0.8 copy.14
  8.0 0.7 reshape.9.columns_ref
  8.6 46.2 %shard_map.55 = bf16[8192,256]{1,0:T(8,128)(2,1)} custom-call(s32[256]{0:T(256)} %reshape.9.columns_ref, s32[1]{0:T(128)S(6)} %copy.32.lengths_ref, bf16[64,4,128,128]{3,2,1,0:T(8,128)(2,1)} %tiles_ref.1, bf16[8192,256]{1,0:T(8,128)(2,1)} %start_ref.1), custom_call_target="tpu_custom_call" | custom-call | tf_op jit(solution)/shard_map/pallas_call | solution.py:150
  54.8 6.2 %copy.15 = bf16[4,2048,256]{1,2,0:T(8,128)(2,1)} copy(bf16[4,2048,256]{2,1,0:T(8,128)(2,1)} %bitcast.18) | data formatting | bytes 8388608 | tf_op jit(solution)/shard_map/all_to_all | solution.py:174
  61.0 94.4 %all_to_all.38 = bf16[4,2048,256]{1,2,0:T(8,128)(2,1)S(1)} all-to-all(bf16[4,2048,256]{1,2,0:T(8,128)(2,1)} %copy.15), channel_id=1, replica_groups=mesh['row'=8,'vec'=4] {'vec'}, dimensions={0} | all-to-all | bytes 8388608 | tf_op jit(solution)/shard_map/all_to_all | solution.py:174
  155.4 0.5 fusion.26
  155.9 0.7 fusion.14
  156.6 1.0 fusion.12
  157.7 1.3 fusion.22
  158.9 1.8 maximum_multiply_fusion
  161.4 138.0 %all-reduce.2.cloned.1.call-done = f32[256,2560]{1,0:T(8,128)} async-done(((f32[256,2560]{1,0:T(8,128)}), f32[256,2560]{1,0:T(8,128)}) %all-reduce.2.cloned.1.call-update) | async-done | bytes 2621456 | tf_op jit(solution)/shard_map/psum | solution.py:190
  299.4 2.6 fusion.33
  302.0 1.8 copy.29
  303.8 1.8 copy.28
  305.6 1.8 copy.27
  307.4 0.8 copy.26
  308.3 0.8 copy.25
  309.1 0.8 copy.30
  310.0 0.1 slice.87
  310.1 0.1 slice.89
  310.2 1.0 copy-done.1
  311.2 0.2 copy-done.10
  311.3 0.3 copy-done.12
  311.6 0.2 copy-done.14
  311.8 0.1 copy-done.15
  311.8 0.1 copy-done.16
  311.9 2.7 select_reduce_fusion
  315.4 11.7 %fusion.21 = f32[1024,1024]{1,0:T(8,128)} fusion(f32[]{:T(128)S(6)} %div.23, f32[256,1024]{1,0:T(8,128)} %copy-done.1, f32[256,256]{1,0:T(8,128)} %bitcast.41, f32[256,768]{1,0:T(8,128)S(1)} %slice.87, f32[256,256]{1,0:T(8,128)} %bitcast.26, f32[256,256]{1,0:T(8,128)} %bitcast.29, f32[256,512]{1,0:T(8,128)} %copy-done.4, f32[256,256]{1,0:T(8,128)} %bitcast.32, ...), kind=kOutput, calls=%fused_computation.24 | convolution fusion | flops 6452936704 | bytes 8388612 | tf_op jit(solution)/shard_map/dot_general | solution.py:204
  327.2 13.1 %divide_convert_fusion = bf16[1024,1024]{1,0:T(8,128)(2,1)} fusion(f32[1024,1024]{1,0:T(8,128)} %fusion.21, f32[]{:T(128)S(6)} %sqrt.3, f32[]{:T(128)S(6)} %div.23, f32[256,1024]{1,0:T(8,128)S(1)} %copy-done.2, f32[256,256]{1,0:T(8,128)} %bitcast.42, f32[256,768]{1,0:T(8,128)S(1)} %slice.87, f32[256,256]{1,0:T(8,128)S(1)} %bitcast.28, ...), kind=kOutput, calls=%fused_computation.1 | convolution fusion | flops 6492782592 | bytes 10485768 | tf_op jit(solution)/shard_map/dot_general | solution.py:208
  340.2 7.4 %convolution_convert_fusion = bf16[2048,1024]{0,1:T(8,128)(2,1)S(1)} fusion(bf16[2048,1024]{0,1:T(8,128)(2,1)} %bitcast.24, bf16[1024,1024]{1,0:T(8,128)(2,1)} %divide_convert_fusion), kind=kOutput, calls=%fused_computation.12 | convolution fusion | flops 4297064448 | bytes 10485760 | tf_op jit(solution)/shard_map/dot_general | solution.py:210
  347.7 95.0 %all_to_all.39 = bf16[2048,4,256]{0,2,1:T(8,128)(2,1)} all-to-all(bf16[2048,4,256]{0,2,1:T(8,128)(2,1)S(1)} %bitcast.25), channel_id=1, replica_groups=mesh['row'=8,'vec'=4] {'vec'}, dimensions={1} | all-to-all | bytes 8388608 | tf_op jit(solution)/shard_map/all_to_all | solution.py:213
  442.7 6.2 %copy.23 = bf16[4,2048,256]{2,1,0:T(8,128)(2,1)} copy(bf16[4,2048,256]{1,2,0:T(8,128)(2,1)} %bitcast.19) | data formatting | bytes 8388608 | tf_op jit(solution)/shard_map/all_to_all | solution.py:213
  (31 shorter events, 0.1 us)
Async XLA Ops:
  6.5 292.9 %all-reduce.2.cloned.1.call-start = ((), (), s32[]{:S(2)}) async-start(), calls=%async_computation.2 | async-start | bytes 5242880 | tf_op jit(solution)/shard_map/psum | solution.py:190
  155.4 2.3 copy-start.3
  299.4 10.5 %copy-start = (f32[256,2560]{1,0:T(8,128)S(1)}, f32[256,2560]{1,0:T(8,128)}, u32[]{:S(2)}) copy-start(f32[256,2560]{1,0:T(8,128)} %all-reduce.2.cloned.1.call-done) | copy-start | bytes 7864324
  309.9 1.2 copy-start.6
  309.9 1.2 copy-start.8
  309.9 1.4 copy-start.10
  309.9 1.7 copy-start.12
  309.9 1.8 copy-start.14
  310.0 1.9 copy-start.15
  310.0 2.0 copy-start.16
  310.0 4.6 %copy-start.4 = (f32[256,512]{1,0:T(8,128)}, f32[256,512]{1,0:T(8,128)S(1)}, u32[]{:S(2)}) copy-start(f32[256,512]{1,0:T(8,128)S(1)} %slice.84) | copy-start | bytes 1572868
  310.2 1.0 copy-start.1
  315.3 11.8 %copy-start.2 = (f32[256,1024]{1,0:T(8,128)S(1)}, f32[256,1024]{1,0:T(8,128)}, u32[]{:S(2)}) copy-start(f32[256,1024]{1,0:T(8,128)} %copy-done.1) | copy-start | bytes 3145732
  315.3 11.8 %copy-start.5 = (f32[256,512]{1,0:T(8,128)S(1)}, f32[256,512]{1,0:T(8,128)}, u32[]{:S(2)}) copy-start(f32[256,512]{1,0:T(8,128)} %copy-done.4) | copy-start | bytes 1572868
  315.4 11.8 %copy-start.7 = (f32[256,256]{1,0:T(8,128)S(1)}, f32[256,256]{1,0:T(8,128)}, u32[]{:S(2)}) copy-start(f32[256,256]{1,0:T(8,128)} %get-tuple-element.5) | copy-start | bytes 786436
  315.4 11.8 %copy-start.9 = (f32[256,256]{0,1:T(8,128)S(1)}, f32[256,256]{0,1:T(8,128)}, u32[]{:S(2)}) copy-start(f32[256,256]{0,1:T(8,128)} %copy.29) | copy-start | bytes 786436
  315.4 11.8 %copy-start.11 = (f32[256,256]{0,1:T(8,128)S(1)}, f32[256,256]{0,1:T(8,128)}, u32[]{:S(2)}) copy-start(f32[256,256]{0,1:T(8,128)} %copy.28) | copy-start | bytes 786436
  315.4 11.8 %copy-start.13 = (f32[256,256]{0,1:T(8,128)S(1)}, f32[256,256]{0,1:T(8,128)}, u32[]{:S(2)}) copy-start(f32[256,256]{0,1:T(8,128)} %copy.27) | copy-start | bytes 786436
Sparse Core Ops, SparseCore 0:
  160.9 138.5 all-reduce.1

commit v2 on v1

--- a/solution.py
+++ b/solution.py
@@ -166,6 +166,116 @@
     )(tile_columns.reshape(-1), stack_lengths, ham_tiles, start_vectors)
 
 
+def gram_sum_kernel(part_ref, out_ref, arrived, outgoing, total, near, thin, far, send_sem, recv_sem):
+    _, quads, panels, _, _ = part_ref.shape
+    row, vec = lax.axis_index("row"), lax.axis_index("vec")
+    side, quad = lax.rem(row, 2), row // 2
+    other = 1 - side
+    partner = quad * 2 + other
+    quad_at = [lax.rem(quad + d, quads) for d in range(quads)]
+    vec_at = [lax.rem(vec + d, panels) for d in range(panels)]
+
+    def ring(axis, places, make):
+        copies = []
+        for d in range(1, len(places)):
+            source, target, slot = make(d)
+            place = places[d] if axis == "vec" else places[d] * 2 + side
+            copies.append(
+                pltpu.make_async_remote_copy(
+                    src_ref=source,
+                    dst_ref=target,
+                    send_sem=send_sem.at[slot],
+                    recv_sem=recv_sem.at[slot],
+                    device_id={axis: place},
+                    device_id_type=pl.DeviceIdType.MESH,
+                )
+            )
+        for copy in copies:
+            copy.start()
+        return copies
+
+    def swap(source, target, slot):
+        copy = pltpu.make_async_remote_copy(
+            src_ref=source,
+            dst_ref=target,
+            send_sem=send_sem.at[slot],
+            recv_sem=recv_sem.at[slot],
+            device_id={"row": partner},
+            device_id_type=pl.DeviceIdType.MESH,
+        )
+        copy.start()
+        copy.wait()
+
+    barrier = pltpu.get_barrier_semaphore()
+    greeted = [{"row": partner}]
+    greeted += [{"row": place * 2 + side} for place in quad_at[1:]]
+    greeted += [{"vec": place} for place in vec_at[1:]]
+    for device in greeted:
+        pl.semaphore_signal(
+            barrier, inc=1, device_id=device, device_id_type=pl.DeviceIdType.MESH
+        )
+    pl.semaphore_wait(barrier, len(greeted))
+
+    slots = iter(range(2 + 2 * (quads - 1) + 2 * (panels - 1)))
+    swap(part_ref.at[other], arrived, next(slots))
+    for d in range(1, quads):
+        place = quad_at[d]
+        outgoing[place] = (part_ref[side, place] + arrived[place]).astype(jnp.bfloat16)
+    total[...] = part_ref[side, quad] + arrived[quad]
+
+    copies = ring(
+        "row", quad_at, lambda d: (outgoing.at[quad_at[d]], near.at[d - 1], next(slots))
+    )
+    for d in range(1, quads):
+        copies[d - 1].wait()
+        total[...] += near[d - 1].astype(jnp.float32)
+
+    thin[...] = total[...].astype(jnp.bfloat16)
+    copies = ring("vec", vec_at, lambda d: (thin.at[vec_at[d]], far.at[d - 1], next(slots)))
+    reduced = total[vec]
+    for d in range(1, panels):
+        copies[d - 1].wait()
+        reduced += far[d - 1].astype(jnp.float32)
+    out_ref[side, quad, vec] = reduced.astype(jnp.bfloat16)
+
+    mine = out_ref.at[side, quad, vec]
+    for copy in ring("vec", vec_at, lambda d: (mine, mine, next(slots))):
+        copy.wait()
+    mine = out_ref.at[side, quad]
+    for copy in ring("row", quad_at, lambda d: (mine, mine, next(slots))):
+        copy.wait()
+    mine = out_ref.at[side]
+    swap(mine, mine, next(slots))
+
+
+def gram_sum(partial):
+    rows, width = partial.shape
+    quads, panels = lax.axis_size("row") // 2, lax.axis_size("vec")
+    height = rows // (2 * quads * panels)
+    copies = 2 + 2 * (quads - 1) + 2 * (panels - 1)
+    vmem = pl.BlockSpec(memory_space=pltpu.VMEM)
+    summed = pl.pallas_call(
+        gram_sum_kernel,
+        out_shape=jax.ShapeDtypeStruct((2, quads, panels, height, width), jnp.bfloat16),
+        in_specs=[vmem],
+        out_specs=vmem,
+        scratch_shapes=[
+            pltpu.VMEM((quads, panels, height, width), jnp.float32),
+            pltpu.VMEM((quads, panels, height, width), jnp.bfloat16),
+            pltpu.VMEM((panels, height, width), jnp.float32),
+            pltpu.VMEM((quads - 1, panels, height, width), jnp.bfloat16),
+            pltpu.VMEM((panels, height, width), jnp.bfloat16),
+            pltpu.VMEM((panels - 1, height, width), jnp.bfloat16),
+            pltpu.SemaphoreType.DMA((copies,)),
+            pltpu.SemaphoreType.DMA((copies,)),
+        ],
+        compiler_params=pltpu.CompilerParams(
+            collective_id=1, has_side_effects=True, vmem_limit_bytes=40 * 1024 * 1024
+        ),
+    )(partial.reshape(2, quads, panels, height, width))
+    return summed.reshape(rows, width)
+
+
 def local(ham_tiles, tile_columns, stack_lengths, start_vectors, spectral_scale):
     row_count, panel_width = start_vectors.shape
     total_rows = row_count * lax.axis_size("row")
@@ -175,37 +285,39 @@
 
     part = 256
     parts = full_width // part
+    pieces = [(i, j) for i in range(parts) for j in range(i + 1)]
     packed = jnp.concatenate(
         [
             lax.dot_general(
+                panel_rows[:, : (j + 1) * part],
                 panel_rows[:, j * part : (j + 1) * part],
-                panel_rows[:, : (j + 1) * part],
                 (((0,), (0,)), ((), ())),
                 preferred_element_type=jnp.float32,
             )
             for j in range(parts)
         ],
-        axis=1,
-    )
-    packed = lax.psum(packed / float(total_rows), ("row", "vec"))
-    starts = [j * (j + 1) // 2 * part for j in range(parts)]
-
-    def block(i, j):
-        if j <= i:
-            return packed[:, starts[i] + j * part : starts[i] + (j + 1) * part]
-        return block(j, i).T
-
+        axis=0,
+    )
+    packed = gram_sum(packed / float(total_rows))
+    blocks = {}
+    for n, (i, j) in enumerate(pieces):
+        blocks[j, i] = packed[n * part : (n + 1) * part]
+        blocks[i, j] = blocks[j, i] if i == j else blocks[j, i].T
     gram = jnp.concatenate(
-        [jnp.concatenate([block(i, j) for j in range(parts)], axis=1) for i in range(parts)], axis=0
-    )
-    scale = spectral_scale[0] * jnp.trace(gram) / full_width
-    system = gram / scale
-    identity = jnp.eye(full_width, dtype=jnp.float32)
-    square = jnp.dot(system, system, precision=lax.Precision.HIGH)
-    first = 1.5 * identity - 0.5 * system
-    left = 1.5 * system - 0.5 * square
-    right = 2.25 * identity - 1.5 * system + 0.25 * square
-    root = 1.5 * first - 0.5 * jnp.dot(left, right, precision=lax.Precision.HIGH)
+        [jnp.concatenate([blocks[i, j] for j in range(parts)], axis=1) for i in range(parts)],
+        axis=0,
+    )
+    identity = jnp.eye(part, dtype=jnp.float32)
+    trace = sum(jnp.sum(blocks[i, i].astype(jnp.float32) * identity) for i in range(parts))
+    scale = spectral_scale[0] * trace / full_width
+    square = jnp.dot(gram, gram, preferred_element_type=jnp.float32) / (scale * scale)
+    system = gram.astype(jnp.float32) / scale
+    root = (
+        2.25 * jnp.eye(full_width, dtype=jnp.float32)
+        - 2.4375 * system
+        + 1.6875 * square
+        + jnp.dot(square, 0.0625 * square - 0.5625 * system, precision=lax.Precision.HIGH)
+    )
     weights = (root / jnp.sqrt(scale)).astype(jnp.bfloat16)
     basis_rows = jnp.dot(panel_rows, weights, preferred_element_type=jnp.float32).astype(
         jnp.bfloat16

time: 461 us -> 349 us (0.76)
  blocking collectives: 189 us -> 94.4 us
  waiting for transfers between devices: 138 us -> 85.8 us
  Pallas kernels: 46.2 us -> 88.9 us
  other arithmetic: 4.51 us -> 16.3 us
  between operations: 15.6 us -> 3.98 us
  local copies, waits for them, and re-layouts: 26.3 us -> 15.3 us
  starting transfers between devices: 0.01 us -> 5.07 us
    psum x1 -> x0, waiting for transfers between devices: 138 us -> none  [local(): packed = lax.psum(packed / float(total_rows), ('row', 'vec'))]
    all_to_all x1 -> x0, blocking collectives: 94.4 us -> none  [local(): lax.all_to_all(current, 'vec', split_axis=0, concat_axis=1, tiled=True)]
    all_to_all x0 -> x1, waiting for transfers between devices: none -> 85.8 us  [local(): lax.all_to_all(current, 'vec', split_axis=0, concat_axis=1, tiled=True)]
    pallas_call x0 -> x1, Pallas kernels: none -> 42.7 us  [gram_sum(): pl.pallas_call(gram_sum_kernel, out_shape=jax.ShapeDtypeStruct((2, quads,...]
    concatenate x0 -> x1, other arithmetic: none -> 15.4 us  [local(): jnp.concatenate([jnp.concatenate([blocks[i, j] for j in range(parts)], ax...]
    unnamed x41 -> x1, local copies, waits for them, and re-layouts: 10.4 us -> 0.77 us
    all_to_all x0 -> x1, starting transfers between devices: none -> 5.07 us  [local(): lax.all_to_all(current, 'vec', split_axis=0, concat_axis=1, tiled=True)]
where the time goes in v2:
time: 349 us; the launch traced here: 345 us
  blocking collectives  94.4 us (27%)
  Pallas kernels  88.9 us (25%)
  waiting for transfers between devices  85.8 us (25%)
  matrix products  34.7 us (10%)
  other arithmetic  16.3 us (5%)
  local copies, waits for them, and re-layouts  15.3 us (4%)
  starting transfers between devices  5.07 us (1%)
  between operations  3.98 us (1%)
    all_to_all x1, blocking collectives, local(): lax.all_to_all(basis_rows, 'vec', split_axis=1, concat_axis=0, tiled=True)  94.4 us
    all_to_all x1, waiting for transfers between devices, local(): lax.all_to_all(current, 'vec', split_axis=0, concat_axis=1, tiled=True)  85.8 us
    pallas_call x1, Pallas kernels, chebyshev(): pl.pallas_call(functools.partial(chebyshev_kernel, block_count * lax.axis...  46.1 us
    pallas_call x1, Pallas kernels, gram_sum(): pl.pallas_call(gram_sum_kernel, out_shape=jax.ShapeDtypeStruct((2, quads,...  42.7 us
    concatenate x1, other arithmetic, local(): jnp.concatenate([jnp.concatenate([blocks[i, j] for j in range(parts)], ax...  15.4 us
    dot_general x1, matrix products, local(): jnp.dot(square, 0.0625 * square - 0.5625 * system, precision=lax.Precisio...  11.8 us
    dot_general x4, matrix products, local(): lax.dot_general(panel_rows[:, :(j + 1) * part], panel_rows[:, j * part:(j...  11.6 us
    dot_general x1, matrix products, local(): jnp.dot(panel_rows, weights, preferred_element_type=jnp.float32)  7.02 us
  transfers between devices with their start and end apart: 1, of which 1 were waited for; matrix products, arithmetic and copies ran while one was open for 0% of the time, Pallas kernels for 0%

profile of v2, /device:TPU:9, one launch (start us, length us, event | category | flops | bytes accessed | tf_op | source)
XLA Modules:
  0.0 344.6 jit_solution(3111787075861705059)
XLA Ops:
  0.7 0.8 copy.13
  1.4 0.7 reshape.16.columns_ref
  2.1 46.1 %shard_map.55 = bf16[8192,256]{1,0:T(8,128)(2,1)} custom-call(s32[256]{0:T(256)} %reshape.16.columns_ref, s32[1]{0:T(128)S(6)} %copy.22.lengths_ref, bf16[64,4,128,128]{3,2,1,0:T(8,128)(2,1)} %tiles_ref.1, bf16[8192,256]{1,0:T(8,128)(2,1)} %start_ref.1), custom_call_target="tpu_custom_call" | custom-call | tf_op jit(solution)/shard_map/pallas_call | solution.py:150
  48.2 6.2 %copy.14 = bf16[4,2048,256]{1,2,0:T(8,128)(2,1)} copy(bf16[4,2048,256]{2,1,0:T(8,128)(2,1)} %bitcast.31) | data formatting | bytes 8388608 | tf_op jit(solution)/shard_map/all_to_all | solution.py:284
  54.4 5.1 %all-to-all-start = ((bf16[4,2048,256]{1,2,0:T(8,128)(2,1)}), bf16[4,2048,256]{1,2,0:T(8,128)(2,1)}, u32[]{:S(2)}, u32[]{:S(2)}) async-start(bf16[4,2048,256]{1,2,0:T(8,128)(2,1)} %copy.14), calls=%async_computation | async-start | bytes 8388608 | tf_op jit(solution)/shard_map/all_to_all | solution.py:284
  60.2 85.8 %all-to-all-done = bf16[4,2048,256]{1,2,0:T(8,128)(2,1)} async-done(((bf16[4,2048,256]{1,2,0:T(8,128)(2,1)}), bf16[4,2048,256]{1,2,0:T(8,128)(2,1)}, u32[]{:S(2)}, u32[]{:S(2)}) %all-to-all-start) | async-done | bytes 4194336 | tf_op jit(solution)/shard_map/all_to_all | solution.py:284
  146.0 2.0 fusion.19
  148.0 2.6 fusion.9
  150.6 3.2 fusion.4
  153.8 3.8 %fusion.15 = f32[1024,256]{1,0:T(8,128)S(1)} fusion(bf16[2048,1024]{0,1:T(8,128)(2,1)} %bitcast.2), kind=kOutput, calls=%fused_computation.19 | convolution fusion | flops 1073741824 | bytes 6291456 | tf_op jit(solution)/shard_map/dot_general | solution.py:291
  157.6 0.2 maximum_multiply_fusion
  157.8 42.7 %shard_map.56 = bf16[2,4,4,80,256]{4,3,2,1,0:T(8,128)(2,1)S(1)} custom-call(f32[2,4,4,80,256]{4,3,2,1,0:T(8,128)S(1)} %bitcast.28), custom_call_target="tpu_custom_call" | custom-call | tf_op jit(solution)/shard_map/pallas_call | solution.py:257
  200.5 0.7 select_reduce_fusion
  201.3 0.9 fusion.23
  204.7 0.1 copy.18
  204.8 0.1 copy.15
  204.9 0.1 copy.17
  205.0 0.1 copy.19
  205.2 0.1 copy.16
  205.3 0.1 copy.20
  205.4 15.4 %maximum_maximum_fusion = bf16[1024,1024]{1,0:T(8,128)(2,1)S(1)} fusion(bf16[256,256]{1,0:T(8,128)(2,1)S(1)} %get-tuple-element.16, bf16[256,256]{1,0:T(8,128)(2,1)S(1)} %copy.20, bf16[256,256]{1,0:T(8,128)(2,1)S(1)} %copy.19, bf16[256,256]{1,0:T(8,128)(2,1)S(1)} %copy.18, bf16[256,256]{1,0:T(8,128)(2,1)S(1)} %get-tuple-element.17, ...), kind=kLoop, calls=%fused_computation.14 | loop fusion | flops 33554432 | bytes 4194304 | tf_op jit(solution)/shard_map/concatenate | solution.py:306
  220.8 4.3 %fusion.24 = f32[1024,1024]{1,0:T(8,128)} fusion(bf16[1024,1024]{1,0:T(8,128)(2,1)S(1)} %maximum_maximum_fusion), kind=kOutput, calls=%fused_computation.39 | convolution fusion | flops 2147483648 | bytes 6291456 | tf_op jit(solution)/shard_map/dot_general | solution.py:313
  225.1 11.8 %divide_convert_fusion = bf16[1024,1024]{1,0:T(8,128)(2,1)S(1)} fusion(bf16[1024,1024]{1,0:T(8,128)(2,1)S(1)} %maximum_maximum_fusion, f32[1024,1024]{1,0:T(8,128)} %fusion.24, f32[]{:T(128)S(6)} %sqrt.3, f32[]{:T(128)S(6)} %mul.60, f32[]{:T(128)S(6)} %div.32), kind=kOutput, calls=%fused_computation | convolution fusion | flops 6462373888 | bytes 8388620 | tf_op jit(solution)/shard_map/dot_general | solution.py:319
  236.9 7.0 %convolution_convert_fusion = bf16[2048,1024]{0,1:T(8,128)(2,1)S(1)} fusion(bf16[2048,1024]{0,1:T(8,128)(2,1)} %bitcast.2, bf16[1024,1024]{1,0:T(8,128)(2,1)S(1)} %divide_convert_fusion), kind=kOutput, calls=%fused_computation.7 | convolution fusion | flops 4297064448 | bytes 10485760 | tf_op jit(solution)/shard_map/dot_general | solution.py:322
  243.9 94.4 %all_to_all.38 = bf16[2048,4,256]{0,2,1:T(8,128)(2,1)} all-to-all(bf16[2048,4,256]{0,2,1:T(8,128)(2,1)S(1)} %bitcast.33), channel_id=1, replica_groups=mesh['row'=8,'vec'=4] {'vec'}, dimensions={1} | all-to-all | bytes 8388608 | tf_op jit(solution)/shard_map/all_to_all | solution.py:325
  338.4 6.2 %copy.21 = bf16[4,2048,256]{2,1,0:T(8,128)(2,1)} copy(bf16[4,2048,256]{1,2,0:T(8,128)(2,1)} %bitcast.32) | data formatting | bytes 8388608 | tf_op jit(solution)/shard_map/all_to_all | solution.py:325
Async XLA Ops:
  54.4 91.5 %all-to-all-start = ((bf16[4,2048,256]{1,2,0:T(8,128)(2,1)}), bf16[4,2048,256]{1,2,0:T(8,128)(2,1)}, u32[]{:S(2)}, u32[]{:S(2)}) async-start(bf16[4,2048,256]{1,2,0:T(8,128)(2,1)} %copy.14), calls=%async_computation | async-start | bytes 8388608 | tf_op jit(solution)/shard_map/all_to_all | solution.py:284

commit v3 on v2

--- a/solution.py
+++ b/solution.py
@@ -21,9 +21,13 @@
     band,
     even,
     odd,
+    final,
     halo,
     send_sem,
     recv_sem,
+    panel_send,
+    panel_recv,
+    keep_sem,
 ):
     block_count, tile_count, tile, _ = tiles_ref.shape
     pair = REACH * tile
@@ -32,13 +36,17 @@
     me = lax.axis_index("row")
     left, right = lax.rem(me + count - 1, count), lax.rem(me + 1, count)
     last = (pairs - 1) * pair
+    vec, panels = lax.axis_index("vec"), lax.axis_size("vec")
+    vec_at = [lax.rem(vec + d, panels) for d in range(panels)]
+    share = pairs // panels
 
     barrier = pltpu.get_barrier_semaphore()
-    for neighbour in (left, right):
+    greeted = [{"row": left}, {"row": right}] + [{"vec": place} for place in vec_at[1:]]
+    for device in greeted:
         pl.semaphore_signal(
-            barrier, inc=1, device_id={"row": neighbour}, device_id_type=pl.DeviceIdType.MESH
-        )
-    pl.semaphore_wait(barrier, 2)
+            barrier, inc=1, device_id=device, device_id_type=pl.DeviceIdType.MESH
+        )
+    pl.semaphore_wait(barrier, len(greeted))
 
     def sends(source, step):
         to_left = pltpu.make_async_remote_copy(
@@ -89,7 +97,7 @@
 
     lax.fori_loop(0, pairs, build, 0)
 
-    held = [start_ref, odd, even, odd, even, odd, out_ref]
+    held = [start_ref] + [(odd, even)[step % 2] for step in range(CHEB - 1)] + [final]
     for step in range(CHEB):
         current, target = held[step], held[step + 1]
         earlier = held[step - 1] if step else None
@@ -132,33 +140,71 @@
             )
             return carry
 
-        early = min(7, pairs - 1)
-        lax.fori_loop(1, early, interior, 0, unroll=3)
         if step < CHEB - 1:
+            early = min(7, pairs - 1)
+            lax.fori_loop(1, early, interior, 0, unroll=3)
             copies = sends(target, step + 1)
             for copy in copies:
                 copy.start()
-        lax.fori_loop(early, pairs - 1, interior, 0, unroll=4)
+            lax.fori_loop(early, pairs - 1, interior, 0, unroll=4)
+
+    def deliver(d):
+        rows = share * pair
+        source = final.at[pl.ds(pl.multiple_of(vec_at[d] * rows, pair), rows)]
+        if d == 0:
+            copy = pltpu.make_async_copy(source, out_ref.at[vec], keep_sem)
+        else:
+            copy = pltpu.make_async_remote_copy(
+                src_ref=source,
+                dst_ref=out_ref.at[vec],
+                send_sem=panel_send.at[d - 1],
+                recv_sem=panel_recv.at[d - 1],
+                device_id={"vec": vec_at[d]},
+                device_id_type=pl.DeviceIdType.MESH,
+            )
+        copy.start()
+        return copy
+
+    order = list(range(1, panels)) + [0]
+    deliveries = []
+    for n, d in enumerate(order):
+
+        def quarter(p, carry):
+            p = vec_at[d] * share + p
+            p = p + lax.div(pairs - 1 - p, pairs - 1) - lax.div(p, pairs - 1)
+            return interior(p, carry)
+
+        lax.fori_loop(0, share, quarter, 0, unroll=4)
+        if n:
+            deliveries.append(deliver(order[n - 1]))
+    deliveries.append(deliver(0))
+    for copy in deliveries:
+        copy.wait()
 
 
 def chebyshev(ham_tiles, tile_columns, stack_lengths, start_vectors):
     block_count, tile_count, tile, _ = ham_tiles.shape
     rows, width = start_vectors.shape
     pair = REACH * tile
+    panels = lax.axis_size("vec")
     vmem = pl.BlockSpec(memory_space=pltpu.VMEM)
     smem = pl.BlockSpec(memory_space=pltpu.SMEM)
     return pl.pallas_call(
         functools.partial(chebyshev_kernel, block_count * lax.axis_size("row")),
-        out_shape=jax.ShapeDtypeStruct((rows, width), jnp.bfloat16),
+        out_shape=jax.ShapeDtypeStruct((panels, rows // panels, width), jnp.bfloat16),
         in_specs=[smem, smem, vmem, vmem],
-        out_specs=vmem,
+        out_specs=pl.BlockSpec(memory_space=pltpu.HBM),
         scratch_shapes=[
             pltpu.VMEM((block_count // REACH, pair, 3 * pair), jnp.bfloat16),
+            pltpu.VMEM((rows, width), jnp.bfloat16),
             pltpu.VMEM((rows, width), jnp.bfloat16),
             pltpu.VMEM((rows, width), jnp.bfloat16),
             pltpu.VMEM((CHEB, 2, pair, width), jnp.bfloat16),
             pltpu.SemaphoreType.DMA((CHEB, 2)),
             pltpu.SemaphoreType.DMA((CHEB, 2)),
+            pltpu.SemaphoreType.DMA((panels - 1,)),
+            pltpu.SemaphoreType.DMA((panels - 1,)),
+            pltpu.SemaphoreType.DMA,
         ],
         compiler_params=pltpu.CompilerParams(
             collective_id=0, has_side_effects=True, vmem_limit_bytes=60 * 1024 * 1024
@@ -276,53 +322,192 @@
     return summed.reshape(rows, width)
 
 
-def local(ham_tiles, tile_columns, stack_lengths, start_vectors, spectral_scale):
-    row_count, panel_width = start_vectors.shape
-    total_rows = row_count * lax.axis_size("row")
-    full_width = panel_width * lax.axis_size("vec")
-    current = chebyshev(ham_tiles, tile_columns, stack_lengths, start_vectors)
-    panel_rows = lax.all_to_all(current, "vec", split_axis=0, concat_axis=1, tiled=True)
-
-    part = 256
-    parts = full_width // part
-    pieces = [(i, j) for i in range(parts) for j in range(i + 1)]
-    packed = jnp.concatenate(
-        [
-            lax.dot_general(
-                panel_rows[:, : (j + 1) * part],
-                panel_rows[:, j * part : (j + 1) * part],
+VMEM = pl.BlockSpec(memory_space=pltpu.VMEM)
+
+
+def gram_parts_kernel(total_rows, panel_ref, out_ref):
+    panels, _, width = panel_ref.shape
+    n = 0
+    for i in range(panels):
+        for j in range(i + 1):
+            product = lax.dot_general(
+                panel_ref[j],
+                panel_ref[i],
                 (((0,), (0,)), ((), ())),
                 preferred_element_type=jnp.float32,
             )
-            for j in range(parts)
+            out_ref[n * width : (n + 1) * width, :] = product / float(total_rows)
+            n += 1
+    tail = out_ref.shape[0] - n * width
+    if tail:
+        out_ref[n * width :, :] = jnp.zeros((tail, width), jnp.float32)
+
+
+def gram_parts(panel_rows, total_rows):
+    panels, _, width = panel_rows.shape
+    unit = 16 * lax.axis_size("row") * panels
+    rows = -(-(panels * (panels + 1) // 2 * width) // unit) * unit
+    return pl.pallas_call(
+        functools.partial(gram_parts_kernel, total_rows),
+        out_shape=jax.ShapeDtypeStruct((rows, width), jnp.float32),
+        in_specs=[VMEM],
+        out_specs=VMEM,
+        compiler_params=pltpu.CompilerParams(vmem_limit_bytes=40 * 1024 * 1024),
+    )(panel_rows)
+
+
+def weights_kernel(spectral_ref, packed_ref, out_ref, gram, high, low, side_high, side_low, base):
+    panels, full, width = out_ref.shape
+    diagonal = lax.broadcasted_iota(jnp.int32, (width, width), 0) == lax.broadcasted_iota(
+        jnp.int32, (width, width), 1
+    )
+    trace = jnp.zeros((1, 1), jnp.float32)
+    n = 0
+    for i in range(panels):
+        for j in range(i + 1):
+            block = packed_ref[n * width : (n + 1) * width, :]
+            n += 1
+            gram[j * width : (j + 1) * width, i * width : (i + 1) * width] = block
+            wide = block.astype(jnp.float32)
+            if i == j:
+                trace += jnp.sum(jnp.where(diagonal, wide, 0.0), axis=(0, 1), keepdims=True)
+            else:
+                gram[i * width : (i + 1) * width, j * width : (j + 1) * width] = wide.T.astype(
+                    jnp.bfloat16
+                )
+    scale = spectral_ref[0] * trace / float(full)
+    inverse = 1.0 / scale
+    shrink = 1.0 / jnp.sqrt(scale)
+
+    def squares(r, carry):
+        rows = pl.ds(pl.multiple_of(r * width, width), width)
+        square = jnp.dot(gram[rows, :], gram[...], preferred_element_type=jnp.float32)
+        square = square * inverse * inverse
+        system = gram[rows, :].astype(jnp.float32) * inverse
+        top = square.astype(jnp.bfloat16)
+        high[rows, :] = top
+        low[rows, :] = (square - top.astype(jnp.float32)).astype(jnp.bfloat16)
+        side = 0.0625 * square - 0.5625 * system
+        top = side.astype(jnp.bfloat16)
+        side_high[rows, :] = top
+        side_low[rows, :] = (side - top.astype(jnp.float32)).astype(jnp.bfloat16)
+        ones = lax.broadcasted_iota(jnp.int32, (width, full), 0) + r * width
+        ones = ones == lax.broadcasted_iota(jnp.int32, (width, full), 1)
+        base[rows, :] = (
+            jnp.where(ones, 2.25, 0.0) - 2.4375 * system + 1.6875 * square
+        )
+        return carry
+
+    lax.fori_loop(0, panels, squares, 0)
+
+    def products(r, carry):
+        rows = pl.ds(pl.multiple_of(r * width, width), width)
+        product = (
+            jnp.dot(high[rows, :], side_high[...], preferred_element_type=jnp.float32)
+            + jnp.dot(high[rows, :], side_low[...], preferred_element_type=jnp.float32)
+            + jnp.dot(low[rows, :], side_high[...], preferred_element_type=jnp.float32)
+        )
+        root = (base[rows, :] + product) * shrink
+        for v in range(panels):
+            out_ref[v, rows, :] = root[:, v * width : (v + 1) * width].astype(jnp.bfloat16)
+        return carry
+
+    lax.fori_loop(0, panels, products, 0)
+
+
+def newton_schulz_weights(packed, spectral_scale, panels):
+    width = packed.shape[1]
+    full = panels * width
+    return pl.pallas_call(
+        weights_kernel,
+        out_shape=jax.ShapeDtypeStruct((panels, full, width), jnp.bfloat16),
+        in_specs=[pl.BlockSpec(memory_space=pltpu.SMEM), VMEM],
+        out_specs=VMEM,
+        scratch_shapes=[pltpu.VMEM((full, full), jnp.bfloat16)] * 5
+        + [pltpu.VMEM((full, full), jnp.float32)],
+        compiler_params=pltpu.CompilerParams(vmem_limit_bytes=50 * 1024 * 1024),
+    )(spectral_scale, packed)
+
+
+def basis_kernel(panel_ref, weights_ref, out_ref, result, send_sem, recv_sem, keep_sem):
+    panels, rows, width = panel_ref.shape
+    vec = lax.axis_index("vec")
+    vec_at = [lax.rem(vec + d, panels) for d in range(panels)]
+    barrier = pltpu.get_barrier_semaphore()
+    for place in vec_at[1:]:
+        pl.semaphore_signal(
+            barrier, inc=1, device_id={"vec": place}, device_id_type=pl.DeviceIdType.MESH
+        )
+    pl.semaphore_wait(barrier, panels - 1)
+    landing = out_ref.at[pl.ds(pl.multiple_of(vec * rows, rows), rows)]
+    chunk = 256
+
+    def deliver(d):
+        source = result.at[vec_at[d]]
+        if d == 0:
+            copy = pltpu.make_async_copy(source, landing, keep_sem)
+        else:
+            copy = pltpu.make_async_remote_copy(
+                src_ref=source,
+                dst_ref=landing,
+                send_sem=send_sem.at[d - 1],
+                recv_sem=recv_sem.at[d - 1],
+                device_id={"vec": vec_at[d]},
+                device_id_type=pl.DeviceIdType.MESH,
+            )
+        copy.start()
+        return copy
+
+    order = list(range(1, panels)) + [0]
+    deliveries = []
+    for n, d in enumerate(order):
+
+        def product(c, carry):
+            here = pl.ds(pl.multiple_of(c * chunk, chunk), chunk)
+            total = None
+            for u in range(panels):
+                term = jnp.dot(
+                    panel_ref[u, here, :],
+                    weights_ref[vec_at[d], u * width : (u + 1) * width, :],
+                    preferred_element_type=jnp.float32,
+                )
+                total = term if total is None else total + term
+            result[vec_at[d], here, :] = total.astype(jnp.bfloat16)
+            return carry
+
+        lax.fori_loop(0, rows // chunk, product, 0, unroll=2)
+        if n:
+            deliveries.append(deliver(order[n - 1]))
+    deliveries.append(deliver(0))
+    for copy in deliveries:
+        copy.wait()
+
+
+def basis(panel_rows, weights):
+    panels, rows, width = panel_rows.shape
+    return pl.pallas_call(
+        basis_kernel,
+        out_shape=jax.ShapeDtypeStruct((panels * rows, width), jnp.bfloat16),
+        in_specs=[VMEM, VMEM],
+        out_specs=pl.BlockSpec(memory_space=pltpu.HBM),
+        scratch_shapes=[
+            pltpu.VMEM((panels, rows, width), jnp.bfloat16),
+            pltpu.SemaphoreType.DMA((panels - 1,)),
+            pltpu.SemaphoreType.DMA((panels - 1,)),
+            pltpu.SemaphoreType.DMA,
         ],
-        axis=0,
-    )
-    packed = gram_sum(packed / float(total_rows))
-    blocks = {}
-    for n, (i, j) in enumerate(pieces):
-        blocks[j, i] = packed[n * part : (n + 1) * part]
-        blocks[i, j] = blocks[j, i] if i == j else blocks[j, i].T
-    gram = jnp.concatenate(
-        [jnp.concatenate([blocks[i, j] for j in range(parts)], axis=1) for i in range(parts)],
-        axis=0,
-    )
-    identity = jnp.eye(part, dtype=jnp.float32)
-    trace = sum(jnp.sum(blocks[i, i].astype(jnp.float32) * identity) for i in range(parts))
-    scale = spectral_scale[0] * trace / full_width
-    square = jnp.dot(gram, gram, preferred_element_type=jnp.float32) / (scale * scale)
-    system = gram.astype(jnp.float32) / scale
-    root = (
-        2.25 * jnp.eye(full_width, dtype=jnp.float32)
-        - 2.4375 * system
-        + 1.6875 * square
-        + jnp.dot(square, 0.0625 * square - 0.5625 * system, precision=lax.Precision.HIGH)
-    )
-    weights = (root / jnp.sqrt(scale)).astype(jnp.bfloat16)
-    basis_rows = jnp.dot(panel_rows, weights, preferred_element_type=jnp.float32).astype(
-        jnp.bfloat16
-    )
-    return lax.all_to_all(basis_rows, "vec", split_axis=1, concat_axis=0, tiled=True)
+        compiler_params=pltpu.CompilerParams(
+            collective_id=2, has_side_effects=True, vmem_limit_bytes=40 * 1024 * 1024
+        ),
+    )(panel_rows, weights)
+
+
+def local(ham_tiles, tile_columns, stack_lengths, start_vectors, spectral_scale):
+    total_rows = start_vectors.shape[0] * lax.axis_size("row")
+    panel_rows = chebyshev(ham_tiles, tile_columns, stack_lengths, start_vectors)
+    packed = gram_sum(gram_parts(panel_rows, total_rows))
+    weights = newton_schulz_weights(packed, spectral_scale, lax.axis_size("vec"))
+    return basis(panel_rows, weights)
 
 
 def solution(mesh):

time: 349 us -> 293 us (0.84); the launches traced: 345 us -> 293 us
  Pallas kernels: 88.9 us -> 286 us
  blocking collectives: 94.4 us -> 0 us
  waiting for transfers between devices: 85.8 us -> 0 us
  matrix products: 34.7 us -> 0 us
  other arithmetic: 16.3 us -> 0 us
  local copies, waits for them, and re-layouts: 15.3 us -> 5.64 us
  starting transfers between devices: 5.07 us -> 0 us
    pallas_call x0 -> x3, Pallas kernels: none -> 114 us  [the longest x1 98.1 us: basis(): pl.pallas_call(basis_kernel, out_shape=jax.ShapeDtypeStruct((panels * row...]
    all_to_all x1 -> x0, blocking collectives: 94.4 us -> none  [local(): lax.all_to_all(basis_rows, 'vec', split_axis=1, concat_axis=0, tiled=True)]
    pallas_call x1, Pallas kernels: 46.1 us -> 136 us  [chebyshev(): pl.pallas_call(functools.partial(chebyshev_kernel, block_count * lax.axis...]
    all_to_all x1 -> x0, waiting for transfers between devices: 85.8 us -> none  [local(): lax.all_to_all(current, 'vec', split_axis=0, concat_axis=1, tiled=True)]
    dot_general x7 -> x0, matrix products: 34.7 us -> none  [the longest x1 11.8 us: local(): jnp.dot(square, 0.0625 * square - 0.5625 * system, precision=lax.Precisio...]
    concatenate x1 -> x0, other arithmetic: 15.4 us -> none  [local(): jnp.concatenate([jnp.concatenate([blocks[i, j] for j in range(parts)], ax...]
    all_to_all x2 -> x0, local copies, waits for them, and re-layouts: 12.4 us -> none  [the longest x1 6.2 us: local(): lax.all_to_all(current, 'vec', split_axis=0, concat_axis=1, tiled=True)]
    pallas_call x1, Pallas kernels: 42.7 us -> 36.1 us  [gram_sum(): pl.pallas_call(gram_sum_kernel, out_shape=jax.ShapeDtypeStruct((2, quads,...]
  transfers between devices with their start and end apart: 1 -> 0, of which waited for: 1 -> 0; matrix products, arithmetic and copies ran while one was open for 0% -> 0% of each run, Pallas kernels for 0% -> 0%
where the time goes in v3:
time: 293 us
  Pallas kernels  286 us (98%)
  local copies, waits for them, and re-layouts  5.64 us (2%)
    pallas_call x1, Pallas kernels, chebyshev(): pl.pallas_call(functools.partial(chebyshev_kernel, block_count * lax.axis...  136 us
    pallas_call x1, Pallas kernels, basis(): pl.pallas_call(basis_kernel, out_shape=jax.ShapeDtypeStruct((panels * row...  98.1 us
    pallas_call x1, Pallas kernels, gram_sum(): pl.pallas_call(gram_sum_kernel, out_shape=jax.ShapeDtypeStruct((2, quads,...  36.1 us
    pallas_call x1, Pallas kernels, newton_schulz_weights(): pl.pallas_call(weights_kernel, out_shape=jax.ShapeDtypeStruct((panels, fu...  12.6 us

profile of v3, /device:TPU:9, one launch (start us, length us, event | category | flops | bytes accessed | tf_op | source)
XLA Modules:
  0.0 293.2 jit_solution(14709951757783752548)
XLA Ops:
  1.3 0.8 copy.6
  2.1 0.7 reshape.9.columns_ref
  2.7 136.4 %shard_map.55.panel_ref = bf16[4,2048,256]{2,1,0:T(8,128)(2,1)} custom-call(s32[256]{0:T(256)} %reshape.9.columns_ref, s32[1]{0:T(128)S(6)} %copy.8.lengths_ref, bf16[64,4,128,128]{3,2,1,0:T(8,128)(2,1)} %tiles_ref.1, bf16[8192,256]{1,0:T(8,128)(2,1)} %start_ref.1), custom_call_target="tpu_custom_call" | custom-call | tf_op jit(solution)/shard_map/pallas_call | solution.py:192
  139.2 0.0 copy-start
  139.2 2.2 copy-done
  141.3 2.9 %shard_map.56 = f32[2560,256]{1,0:T(8,128)S(1)} custom-call(bf16[4,2048,256]{2,1,0:T(8,128)(2,1)S(1)} %copy-done), custom_call_target="tpu_custom_call" | custom-call | tf_op jit(solution)/shard_map/pallas_call | solution.py:350
  144.3 0.0 copy-start.1
  144.3 36.1 %shard_map.57 = bf16[2,4,4,80,256]{4,3,2,1,0:T(8,128)(2,1)S(1)} custom-call(f32[2,4,4,80,256]{4,3,2,1,0:T(8,128)S(1)} %bitcast.2), custom_call_target="tpu_custom_call" | custom-call | tf_op jit(solution)/shard_map/pallas_call | solution.py:303
  180.4 12.6 %shard_map.58.weights_ref = bf16[4,1024,256]{2,1,0:T(8,128)(2,1)S(1)} custom-call(f32[1]{0:T(128)S(6)} %copy.9.spectral_ref, bf16[2560,256]{1,0:T(8,128)(2,1)S(1)} %bitcast.3), custom_call_target="tpu_custom_call" | custom-call | tf_op jit(solution)/shard_map/pallas_call | solution.py:421
  193.0 0.0 copy-done.1
  193.0 98.1 %shard_map.59 = bf16[8192,256]{1,0:T(8,128)(2,1)S(1)} custom-call(bf16[4,2048,256]{2,1,0:T(8,128)(2,1)S(1)} %copy-done.1, bf16[4,1024,256]{2,1,0:T(8,128)(2,1)S(1)} %shard_map.58.weights_ref), custom_call_target="tpu_custom_call" | custom-call | tf_op jit(solution)/shard_map/pallas_call | solution.py:488
  291.2 2.0 copy.10
Async XLA Ops:
  139.2 2.2 copy-start
  144.3 48.7 %copy-start.1 = (bf16[4,2048,256]{2,1,0:T(8,128)(2,1)S(1)}, bf16[4,2048,256]{2,1,0:T(8,128)(2,1)}, u32[]{:S(2)}) copy-start(bf16[4,2048,256]{2,1,0:T(8,128)(2,1)} %shard_map.55.panel_ref) | copy-start | bytes 12582916

commit v4 on v3

--- a/solution.py
+++ b/solution.py
@@ -98,26 +98,65 @@
     lax.fori_loop(0, pairs, build, 0)
 
     held = [start_ref] + [(odd, even)[step % 2] for step in range(CHEB - 1)] + [final]
+
+    def finish(step, product, rows):
+        if step:
+            product = 2.0 * product - held[step - 1][rows, :].astype(jnp.float32)
+        held[step + 1][rows, :] = product.astype(jnp.bfloat16)
+
+    def interior(step, p):
+        before = pl.multiple_of((p - 1) * pair, pair)
+        here = pl.multiple_of(p * pair, pair)
+        finish(
+            step,
+            jnp.dot(
+                band[p], held[step][pl.ds(before, 3 * pair), :], preferred_element_type=jnp.float32
+            ),
+            pl.ds(here, pair),
+        )
+
+    def deliver(d):
+        rows = share * pair
+        source = final.at[pl.ds(pl.multiple_of(vec_at[d] * rows, pair), rows)]
+        if d == 0:
+            return pltpu.make_async_copy(source, out_ref.at[vec], keep_sem)
+        return pltpu.make_async_remote_copy(
+            src_ref=source,
+            dst_ref=out_ref.at[vec],
+            send_sem=panel_send.at[d - 1],
+            recv_sem=panel_recv.at[d - 1],
+            device_id={"vec": vec_at[d]},
+            device_id_type=pl.DeviceIdType.MESH,
+        )
+
+    order = list(range(1, panels)) + [0]
+    deliveries = [deliver(d) for d in order]
+    outer = panels // 4
+    central = [(vec_at[d] >= outer) & (vec_at[d] < panels - outer) for d in order]
+
+    edge = max(outer * share - CHEB + 1, 1)
     for step in range(CHEB):
-        current, target = held[step], held[step + 1]
-        earlier = held[step - 1] if step else None
-
-        def finish(product, rows):
-            if earlier is not None:
-                product = 2.0 * product - earlier[rows, :].astype(jnp.float32)
-            target[rows, :] = product.astype(jnp.bfloat16)
-
+
+        def centre(p, carry, step=step):
+            interior(step, p)
+            return carry
+
+        lax.fori_loop(edge + step, pairs - edge - step, centre, 0, unroll=2)
+
+    for step in range(CHEB):
+        current = held[step]
         for copy in copies:
             copy.wait()
-        top = pl.ds(0, pair)
         finish(
+            step,
             jnp.dot(band[0, :, :pair], halo[step, 0], preferred_element_type=jnp.float32)
             + jnp.dot(
                 band[0, :, pair:], current[0 : 2 * pair, :], preferred_element_type=jnp.float32
             ),
-            top,
+            pl.ds(0, pair),
         )
         finish(
+            step,
             jnp.dot(
                 band[pairs - 1, :, 2 * pair :], halo[step, 1], preferred_element_type=jnp.float32
             )
@@ -129,55 +168,24 @@
             pl.ds(last, pair),
         )
 
-        def interior(p, carry):
-            before = pl.multiple_of((p - 1) * pair, pair)
-            here = pl.multiple_of(p * pair, pair)
-            finish(
-                jnp.dot(
-                    band[p], current[pl.ds(before, 3 * pair), :], preferred_element_type=jnp.float32
-                ),
-                pl.ds(here, pair),
-            )
+        def sides(p, carry, step=step):
+            interior(step, p)
+            interior(step, pairs - 1 - p)
             return carry
 
+        begin = min(2, edge + step)
+        lax.fori_loop(1, begin, sides, 0)
         if step < CHEB - 1:
-            early = min(7, pairs - 1)
-            lax.fori_loop(1, early, interior, 0, unroll=3)
-            copies = sends(target, step + 1)
+            copies = sends(held[step + 1], step + 1)
             for copy in copies:
                 copy.start()
-            lax.fori_loop(early, pairs - 1, interior, 0, unroll=4)
-
-    def deliver(d):
-        rows = share * pair
-        source = final.at[pl.ds(pl.multiple_of(vec_at[d] * rows, pair), rows)]
-        if d == 0:
-            copy = pltpu.make_async_copy(source, out_ref.at[vec], keep_sem)
-        else:
-            copy = pltpu.make_async_remote_copy(
-                src_ref=source,
-                dst_ref=out_ref.at[vec],
-                send_sem=panel_send.at[d - 1],
-                recv_sem=panel_recv.at[d - 1],
-                device_id={"vec": vec_at[d]},
-                device_id_type=pl.DeviceIdType.MESH,
-            )
-        copy.start()
-        return copy
-
-    order = list(range(1, panels)) + [0]
-    deliveries = []
-    for n, d in enumerate(order):
-
-        def quarter(p, carry):
-            p = vec_at[d] * share + p
-            p = p + lax.div(pairs - 1 - p, pairs - 1) - lax.div(p, pairs - 1)
-            return interior(p, carry)
-
-        lax.fori_loop(0, share, quarter, 0, unroll=4)
-        if n:
-            deliveries.append(deliver(order[n - 1]))
-    deliveries.append(deliver(0))
+        if step == 0:
+            for ready, copy in zip(central, deliveries):
+                pl.when(ready)(copy.start)
+        lax.fori_loop(begin, edge + step, sides, 0)
+
+    for ready, copy in zip(central, deliveries):
+        pl.when(jnp.logical_not(ready))(copy.start)
     for copy in deliveries:
         copy.wait()
 

time: 293 us -> 292 us (level)
    pallas_call x1, Pallas kernels: 136 us -> 130 us  [chebyshev(): pl.pallas_call(functools.partial(chebyshev_kernel, block_count * lax.axis...]
    pallas_call x1, Pallas kernels: 36.1 us -> 40.2 us  [gram_sum(): pl.pallas_call(gram_sum_kernel, out_shape=jax.ShapeDtypeStruct((2, quads,...]
where the time goes in v4:
time: 292 us; the launch traced here: 291 us
  Pallas kernels  284 us (97%)
  local copies, waits for them, and re-layouts  5.64 us (2%)
    pallas_call x1, Pallas kernels, chebyshev(): pl.pallas_call(functools.partial(chebyshev_kernel, block_count * lax.axis...  130 us
    pallas_call x1, Pallas kernels, basis(): pl.pallas_call(basis_kernel, out_shape=jax.ShapeDtypeStruct((panels * row...  97.7 us
    pallas_call x1, Pallas kernels, gram_sum(): pl.pallas_call(gram_sum_kernel, out_shape=jax.ShapeDtypeStruct((2, quads,...  40.2 us
    pallas_call x1, Pallas kernels, newton_schulz_weights(): pl.pallas_call(weights_kernel, out_shape=jax.ShapeDtypeStruct((panels, fu...  12.4 us

profile of v4, /device:TPU:9, one launch (start us, length us, event | category | flops | bytes accessed | tf_op | source)
XLA Modules:
  0.0 290.8 jit_solution(7933407996179129283)
XLA Ops:
  1.3 0.8 copy.6
  2.1 0.7 reshape.9.columns_ref
  2.7 130.5 %shard_map.55.panel_ref = bf16[4,2048,256]{2,1,0:T(8,128)(2,1)} custom-call(s32[256]{0:T(256)} %reshape.9.columns_ref, s32[1]{0:T(128)S(6)} %copy.8.lengths_ref, bf16[64,4,128,128]{3,2,1,0:T(8,128)(2,1)} %tiles_ref.1, bf16[8192,256]{1,0:T(8,128)(2,1)} %start_ref.1), custom_call_target="tpu_custom_call" | custom-call | tf_op jit(solution)/shard_map/pallas_call | solution.py:200
  133.2 0.0 copy-start
  133.3 2.2 copy-done
  135.4 2.9 %shard_map.56 = f32[2560,256]{1,0:T(8,128)S(1)} custom-call(bf16[4,2048,256]{2,1,0:T(8,128)(2,1)S(1)} %copy-done), custom_call_target="tpu_custom_call" | custom-call | tf_op jit(solution)/shard_map/pallas_call | solution.py:358
  138.4 0.0 copy-start.1
  138.4 40.2 %shard_map.57 = bf16[2,4,4,80,256]{4,3,2,1,0:T(8,128)(2,1)S(1)} custom-call(f32[2,4,4,80,256]{4,3,2,1,0:T(8,128)S(1)} %bitcast.2), custom_call_target="tpu_custom_call" | custom-call | tf_op jit(solution)/shard_map/pallas_call | solution.py:311
  178.6 12.4 %shard_map.58.weights_ref = bf16[4,1024,256]{2,1,0:T(8,128)(2,1)S(1)} custom-call(f32[1]{0:T(128)S(6)} %copy.9.spectral_ref, bf16[2560,256]{1,0:T(8,128)(2,1)S(1)} %bitcast.3), custom_call_target="tpu_custom_call" | custom-call | tf_op jit(solution)/shard_map/pallas_call | solution.py:429
  191.0 0.0 copy-done.1
  191.1 97.7 %shard_map.59 = bf16[8192,256]{1,0:T(8,128)(2,1)S(1)} custom-call(bf16[4,2048,256]{2,1,0:T(8,128)(2,1)S(1)} %copy-done.1, bf16[4,1024,256]{2,1,0:T(8,128)(2,1)S(1)} %shard_map.58.weights_ref), custom_call_target="tpu_custom_call" | custom-call | tf_op jit(solution)/shard_map/pallas_call | solution.py:496
  288.7 2.0 copy.10
Async XLA Ops:
  133.2 2.2 copy-start
  138.4 52.7 %copy-start.1 = (bf16[4,2048,256]{2,1,0:T(8,128)(2,1)S(1)}, bf16[4,2048,256]{2,1,0:T(8,128)(2,1)}, u32[]{:S(2)}) copy-start(bf16[4,2048,256]{2,1,0:T(8,128)(2,1)} %shard_map.55.panel_ref) | copy-start | bytes 12582916
